TPU v7x, 128 devices: a whole 4x4x4 slice. The times are simulated.
128 devices in a mesh: sym: 8 (over y, x_lo), row: 16 (over x_hi, z, core).
Axes of the slice: x: 4 (x_hi: 2, x_lo: 2; x = x_hi * 2 + x_lo), y: 4, z: 4, core: 2. Of those that a mesh axis runs over, the one named last changes fastest.
Arguments:
- inner_state: float32 [8, 6144, 128], P('sym', 'row'), may hold values from -6 to 6
- outer_state: float32 [8, 24, 128, 2048], P('sym', None, None, 'row'), may hold values from -6 to 6
- block_hamiltonian: bfloat16 [8, 6144, 6144], P('sym', 'row'), may hold values from -2 to 2, as said below
- dipole: bfloat16 [8, 6144, 6144], P('sym', 'row'), may hold values from -0.078125 to 0.078125
- field_strength: float32 [64], replicated, may hold values from -1.2 to 1.2
- dipole_links: int32 [7, 64], replicated, may hold values 0 or 1
- ghost_amplitude: float32 [8, 2, 6144], P('sym'), may hold values from -0.4 to 0.4
- surface_amplitude: float32 [8, 6144], P('sym'), may hold values from -3 to 3
- state_channel: int32 [8, 6144], P('sym'), may hold values from 0 to 23
- threshold: float32 [8, 24], P('sym'), may hold values from 0 to 1
Outputs:
- inner_next: float32 [8, 6144, 128], P('sym', 'row')
- outer_next: float32 [8, 24, 128, 2048], P('sym', None, None, 'row')
Inputs may be any that keep to these rules, and one draw needn't show every extreme that they name: `block_hamiltonian`: each block is a symmetric matrix.
All inputs are finite; a program needn't handle non-finite values.
Results may differ from a plain program's by a relative error of at most 0.0085.
Values may be sent and summed in bfloat16 or wider, within the bound.
A program may use at most 128 MiB of HBM per device.

v0:
```python
import jax
import jax.numpy as jnp
from jax import lax
from jax.sharding import PartitionSpec as P

TERMS = 4
time_step = 2.0
spacing = 1.5
radius_start = 20.0
charge = 1.0


def shifted(x, axis, by):
    length = lax.axis_size(axis)
    pairs = [(i, i + by) for i in range(length) if 0 <= i + by < length]
    return lax.ppermute(x, axis, pairs)


def padded_2(block, sides, width):
    for axis, dim in sides:
        count = lax.axis_size(axis)
        forward = [(i, i + 1) for i in range(count - 1)]
        backward = [(target, source) for source, target in forward]
        low = lax.ppermute(
            lax.slice_in_dim(block, block.shape[dim] - width, None, axis=dim), axis, forward
        )
        high = lax.ppermute(lax.slice_in_dim(block, 0, width, axis=dim), axis, backward)
        block = jnp.concatenate([low, block, high], axis=dim)
    return block


def from_root(x, axis, root):
    return lax.dynamic_index_in_dim(lax.all_gather(x, axis), root, 0, keepdims=False)


def rotate(values, factor, axis):
    real_part, imag_part = jnp.split(values, 2, axis=axis)
    return jnp.concatenate([factor * imag_part, -factor * real_part], axis=axis)


def per_device(
    inner_state,
    outer_state,
    block_hamiltonian,
    dipole,
    field_strength,
    dipole_links,
    ghost_amplitude,
    surface_amplitude,
    state_channel,
    threshold,
):
    hamiltonian_rows = block_hamiltonian[0]
    dipole_rows = dipole[0]
    rows_here, all_states = hamiltonian_rows.shape
    channel_count = threshold.shape[1]
    radial_here = outer_state.shape[3]
    block_index = lax.axis_index("sym")
    row_index = lax.axis_index("row")
    block_total = dipole_links.shape[0] + 1
    link_row = lax.dynamic_index_in_dim(
        dipole_links, jnp.minimum(block_index, block_total - 2), 0, keepdims=False
    ).astype(jnp.float32)
    link_row = jnp.where(block_index == block_total - 1, jnp.zeros_like(link_row), link_row)
    coupled = jnp.concatenate([link_row, link_row])
    column_field = jnp.concatenate([field_strength, field_strength])
    channel_hot = (
        state_channel[0][:, None] == jnp.arange(channel_count, dtype=jnp.int32)[None, :]
    ).astype(jnp.float32)
    own_hot = lax.dynamic_slice_in_dim(channel_hot, row_index * rows_here, rows_here, 0)
    own_surface = lax.dynamic_slice_in_dim(
        surface_amplitude[0], row_index * rows_here, rows_here, 0
    )
    ghost_rows = ghost_amplitude[0]
    radius = radius_start + spacing * (
        row_index * radial_here + jnp.arange(radial_here, dtype=jnp.int32)
    ).astype(jnp.float32)
    potential = threshold[0][:, None] - charge / radius[None, :]
    first_slab = row_index == 0
    dipole_cols = None
    dipole_cols = lax.all_to_all(dipole_rows, "row", split_axis=1, concat_axis=0, tiled=True)
    inner_vec = inner_state[0]
    outer_vec = outer_state[0]
    inner_total = inner_vec
    outer_total = outer_vec
    for order in range(1, TERMS + 1):
        rounded = inner_vec.astype(jnp.bfloat16)
        from_above = shifted(rounded, "sym", -1)
        own_piece = lax.all_gather(rounded, "row", axis=0, tiled=True)
        upper_piece = lax.all_gather(from_above, "row", axis=0, tiled=True)
        hamiltonian_part = jnp.dot(hamiltonian_rows, own_piece, preferred_element_type=jnp.float32)
        upper_part = jnp.dot(dipole_rows, upper_piece, preferred_element_type=jnp.float32)
        weighted = channel_hot[None, :, :] * ghost_rows[:, :, None]
        ghost = jnp.einsum(
            "jpc,pq->jcq", weighted, own_piece.astype(jnp.float32), precision=lax.Precision.HIGHEST
        )
        lifted = lax.dot_general(
            dipole_cols, own_piece, (((0,), (0,)), ((), ())), preferred_element_type=jnp.float32
        )
        hamiltonian_part, upper_part, ghost, lifted = (hamiltonian_part, upper_part, ghost, lifted)
        lifted = lifted * coupled[None, :]
        lower_part = shifted(lifted.astype(jnp.bfloat16), "sym", 1).astype(lifted.dtype)
        padded = padded_2(outer_vec.astype(jnp.bfloat16), (("row", 2),), 2).astype(outer_vec.dtype)
        ghost_cols = jnp.stack([ghost[1], ghost[0]], axis=-1)
        lower_cols = jnp.where(first_slab, ghost_cols, padded[..., :2])
        padded = jnp.concatenate([lower_cols, padded[..., 2:]], axis=-1)
        laplace = (
            -padded[..., :-4]
            + 16.0 * padded[..., 1:-3]
            - 30.0 * padded[..., 2:-2]
            + 16.0 * padded[..., 3:-1]
            - padded[..., 4:]
        ) / (12.0 * spacing * spacing)
        outer_image = -0.5 * laplace + potential[:, None, :] * outer_vec
        slope = (outer_vec[..., 1] - ghost[0]) / (2.0 * spacing)
        slope = from_root(slope, "row", 0)
        source = jnp.dot(own_hot, slope, precision=lax.Precision.HIGHEST)
        inner_image = (
            hamiltonian_part
            + column_field[None, :] * (coupled[None, :] * upper_part + lower_part)
            + 0.5 * own_surface[:, None] * source
        )
        factor = time_step / order
        inner_vec = rotate(inner_image, factor, 1)
        outer_vec = rotate(outer_image, factor, 1)
        inner_total = inner_total + inner_vec
        outer_total = outer_total + outer_vec
    return (inner_total[None], outer_total[None])


def solution(mesh):
    return jax.shard_map(
        per_device,
        mesh=mesh,
        in_specs=(
            P("sym", "row", None),
            P("sym", None, None, "row"),
            P("sym", "row", None),
            P("sym", "row", None),
            P(),
            P(),
            P("sym", None, None),
            P("sym", None),
            P("sym", None),
            P("sym", None),
        ),
        out_specs=(P("sym", "row", None), P("sym", None, None, "row")),
        check_vma=False,
    )
```

profile of v0, /device:TPU:1, one launch (start us, length us, event | category | flops | bytes accessed | tf_op | source)
XLA Modules:
  0.0 454.4 jit_solution(4584209563427411953)
XLA Ops:
  8.8 6.6 %copy.41 = bf16[1,384,6144]{1,2,0:T(8,128)(2,1)} copy(bf16[1,384,6144]{2,1,0:T(8,128)(2,1)} %param.13) | data formatting | bytes 9437184 | tf_op args[3]
  15.5 9.4 %all-to-all-start = ((bf16[384,16,384]{0,2,1:T(8,128)(2,1)}), bf16[384,16,384]{0,2,1:T(8,128)(2,1)}, u32[]{:S(2)}, u32[]{:S(2)}) async-start(bf16[384,16,384]{0,2,1:T(8,128)(2,1)} %bitcast.245), calls=%async_computation | async-start | bytes 9437184 | tf_op jit(solution)/shard_map/all_to_all | solution.py:81
  29.0 62.2 %collective-permute-done = bf16[384,128]{1,0:T(8,128)(2,1)} collective-permute-done((bf16[384,128]{1,0:T(8,128)(2,1)}, bf16[384,128]{1,0:T(8,128)(2,1)}, u32[]{:S(2)}, u32[]{:S(2)}) %collective-permute-start) | collective-permute-done | bytes 98336 | tf_op jit(solution)/shard_map/ppermute | solution.py:16
  92.1 8.6 %all-gather.24.cloned.1.call-done = bf16[1,6144,128]{2,1,0:T(8,128)(2,1)} async-done(((bf16[1,384,128]{2,1,0:T(8,128)(2,1)}), bf16[1,6144,128]{2,1,0:T(8,128)(2,1)}) %all-gather.24.cloned.1.call-update) | async-done | bytes 1572880 | tf_op jit(solution)/shard_map/all_gather | solution.py:89
  103.0 27.1 %all_gather.42 = f32[16,24,128]{2,1,0:T(8,128)} all-gather(f32[1,24,128]{2,1,0:T(8,128)S(1)} %get-tuple-element.56), channel_id=1, replica_groups=mesh['sym'=8,'row'=16] {'row'}, dimensions={0}, use_global_device_ids=true | all-gather | bytes 208896 | tf_op jit(solution)/shard_map/all_gather | solution.py:33
  130.2 4.5 fusion.14
  134.7 6.8 %copy.42 = bf16[16,384,384]{2,1,0:T(8,128)(2,1)} copy(bf16[16,384,384]{1,2,0:T(8,128)(2,1)} %bitcast.6) | data formatting | bytes 9437184 | tf_op jit(solution)/shard_map/all_to_all | solution.py:81
  141.4 4.0 fusion.156
  145.5 3.6 collective-permute-start.1
  150.1 4.3 all-gather.10.cloned.1.call-done
  154.3 4.3 fusion.123
  162.1 3.0 collective-permute-start.4
  174.5 29.3 %all-gather.12.cloned.1.call-done = bf16[6144,128]{0,1:T(8,128)(2,1)} async-done(((bf16[384,128]{0,1:T(8,128)(2,1)}), bf16[6144,128]{0,1:T(8,128)(2,1)}) %all-gather.12.cloned.1.call-update) | async-done | bytes 1572880 | tf_op jit(solution)/shard_map/all_gather | solution.py:89
  203.8 3.9 fusion.161
  212.5 23.1 %all_gather.45 = f32[16,24,128]{2,1,0:T(8,128)S(1)} all-gather(f32[1,24,128]{2,1,0:T(8,128)S(1)} %get-tuple-element.53), channel_id=1, replica_groups=mesh['sym'=8,'row'=16] {'row'}, dimensions={0}, use_global_device_ids=true | all-gather | bytes 208896 | tf_op jit(solution)/shard_map/all_gather | solution.py:33
  235.7 4.5 fusion.75
  241.9 8.1 %all-gather.14.cloned.1.call-done = bf16[6144,128]{0,1:T(8,128)(2,1)} async-done(((bf16[384,128]{0,1:T(8,128)(2,1)}), bf16[6144,128]{0,1:T(8,128)(2,1)}) %all-gather.14.cloned.1.call-update) | async-done | bytes 1572880 | tf_op jit(solution)/shard_map/all_gather | solution.py:90
  250.0 4.4 fusion.132
  257.2 5.1 %collective-permute-done.6 = bf16[384,128]{0,1:T(8,128)(2,1)} collective-permute-done((bf16[384,128]{0,1:T(8,128)(2,1)}, bf16[384,128]{0,1:T(8,128)(2,1)}, u32[]{:S(2)}, u32[]{:S(2)}) %collective-permute-start.6) | collective-permute-done | bytes 98336 | tf_op jit(solution)/shard_map/ppermute | solution.py:16
  268.9 3.1 collective-permute-done.9
  277.6 22.3 %all-gather.16.cloned.1.call-done = bf16[6144,128]{0,1:T(8,128)(2,1)} async-done(((bf16[384,128]{0,1:T(8,128)(2,1)}), bf16[6144,128]{0,1:T(8,128)(2,1)}) %all-gather.16.cloned.1.call-update) | async-done | bytes 1572880 | tf_op jit(solution)/shard_map/all_gather | solution.py:89
  299.9 4.6 %fusion.160 = bf16[384,128]{0,1:T(8,128)(2,1)} fusion(bf16[6144,128]{0,1:T(8,128)(2,1)} %all-gather.16.cloned.1.call-done, bf16[6144,384]{1,0:T(8,128)(2,1)} %bitcast.242, f32[128]{0:T(128)S(1)} %pad_maximum_fusion.11), kind=kOutput, calls=%fused_computation.148 | convolution fusion | flops 604078080 | bytes 6390272 | tf_op jit(solution)/shard_map/dot_general | solution.py:97
  309.2 22.9 %all_gather.48 = f32[16,24,128]{2,1,0:T(8,128)S(1)} all-gather(f32[1,24,128]{2,1,0:T(8,128)S(1)} %get-tuple-element.50), channel_id=1, replica_groups=mesh['sym'=8,'row'=16] {'row'}, dimensions={0}, use_global_device_ids=true | all-gather | bytes 208896 | tf_op jit(solution)/shard_map/all_gather | solution.py:33
  332.2 4.5 fusion.78
  338.4 7.8 %all-gather.18.cloned.1.call-done = bf16[6144,128]{0,1:T(8,128)(2,1)} async-done(((bf16[384,128]{0,1:T(8,128)(2,1)}), bf16[6144,128]{0,1:T(8,128)(2,1)}) %all-gather.18.cloned.1.call-update) | async-done | bytes 1572880 | tf_op jit(solution)/shard_map/all_gather | solution.py:90
  346.1 4.4 fusion.141
  378.2 17.8 %all-gather.20.cloned.1.call-done = bf16[6144,128]{0,1:T(8,128)(2,1)} async-done(((bf16[384,128]{0,1:T(8,128)(2,1)}), bf16[6144,128]{0,1:T(8,128)(2,1)}) %all-gather.20.cloned.1.call-update) | async-done | bytes 1572880 | tf_op jit(solution)/shard_map/all_gather | solution.py:89
  396.0 4.6 %fusion.159 = bf16[384,128]{0,1:T(8,128)(2,1)} fusion(bf16[6144,128]{0,1:T(8,128)(2,1)} %all-gather.20.cloned.1.call-done, bf16[6144,384]{1,0:T(8,128)(2,1)} %bitcast.243, f32[128]{0:T(128)S(1)} %pad_maximum_fusion.11), kind=kOutput, calls=%fused_computation.147 | convolution fusion | flops 604078080 | bytes 6390272 | tf_op jit(solution)/shard_map/dot_general | solution.py:97
  400.6 3.0 collective-permute-start.11
  405.4 23.1 %all_gather.51 = f32[16,24,128]{2,1,0:T(8,128)S(1)} all-gather(f32[1,24,128]{2,1,0:T(8,128)S(1)} %get-tuple-element.47), channel_id=1, replica_groups=mesh['sym'=8,'row'=16] {'row'}, dimensions={0}, use_global_device_ids=true | all-gather | bytes 208896 | tf_op jit(solution)/shard_map/all_gather | solution.py:33
  438.4 3.9 all-gather.22.cloned.1.call-done
  442.2 4.3 fusion.150
  (201 shorter events, 90.4 us)
Async XLA Ops:
  7.2 93.5 %all-gather.24.cloned.1.call-start = ((), (), s32[]{:S(2)}) async-start(), calls=%async_computation.8 | async-start | bytes 1671168 | tf_op jit(solution)/shard_map/all_gather | solution.py:89
  15.5 119.2 %all-to-all-start = ((bf16[384,16,384]{0,2,1:T(8,128)(2,1)}), bf16[384,16,384]{0,2,1:T(8,128)(2,1)}, u32[]{:S(2)}, u32[]{:S(2)}) async-start(bf16[384,16,384]{0,2,1:T(8,128)(2,1)} %bitcast.245), calls=%async_computation | async-start | bytes 9437184 | tf_op jit(solution)/shard_map/all_to_all | solution.py:81
  24.9 129.4 %all-gather.10.cloned.1.call-start = ((), (), s32[]{:S(2)}) async-start(), calls=%async_computation.1 | async-start | bytes 1671168 | tf_op jit(solution)/shard_map/all_gather | solution.py:90
  25.6 65.6 %collective-permute-start = (bf16[384,128]{1,0:T(8,128)(2,1)}, bf16[384,128]{1,0:T(8,128)(2,1)}, u32[]{:S(2)}, u32[]{:S(2)}) collective-permute-start(bf16[384,128]{1,0:T(8,128)(2,1)} %convert_bitcast_fusion), channel_id=1, source_target_pairs={{16,0},{32,16},{48,32},{64,48},{80,64},{96,80},{112,96},{17,1},{33... | collective-permute-start | bytes 294920 | tf_op jit(solution)/shard_map/ppermute | solution.py:16
  26.9 64.4 %copy-start.41 = (s32[1,6144]{1,0:T(1,128)S(1)}, s32[1,6144]{1,0:T(1,128)}, u32[]{:S(2)}) copy-start(s32[1,6144]{1,0:T(1,128)} %param.18) | copy-start | bytes 73732
  26.9 73.7 %copy-start.30 = (f32[1,2,6144]{2,1,0:T(2,128)S(1)}, f32[1,2,6144]{2,1,0:T(2,128)}, u32[]{:S(2)}) copy-start(f32[1,2,6144]{2,1,0:T(2,128)} %param.16) | copy-start | bytes 147460
  91.2 112.6 %all-gather.12.cloned.1.call-start = ((), (), s32[]{:S(2)}) async-start(), calls=%async_computation.2 | async-start | bytes 1671168 | tf_op jit(solution)/shard_map/all_gather | solution.py:89
  92.1 42.6 %copy-start.10 = (f32[6144,24]{0,1:T(8,128)}, f32[6144,24]{0,1:T(8,128)S(1)}, u32[]{:S(2)}) copy-start(f32[6144,24]{0,1:T(8,128)S(1)} %get-tuple-element.58) | copy-start | bytes 1769476
  100.7 29.5 %copy-start.19 = (bf16[1,6144,128]{2,1,0:T(8,128)(2,1)S(1)}, bf16[1,6144,128]{2,1,0:T(8,128)(2,1)}, u32[]{:S(2)}) copy-start(bf16[1,6144,128]{2,1,0:T(8,128)(2,1)} %all-gather.24.cloned.1.call-done) | copy-start | bytes 4718596
  145.5 8.9 %collective-permute-start.1 = (bf16[384,128]{0,1:T(8,128)(2,1)}, bf16[384,128]{0,1:T(8,128)(2,1)S(1)}, u32[]{:S(2)}, u32[]{:S(2)}) collective-permute-start(bf16[384,128]{0,1:T(8,128)(2,1)} %fusion.156), channel_id=1, source_target_pairs={{0,16},{16,32},{32,48},{48,64},{64,80},{80,96},{96,112},{1,17},{17... | collective-permute-start | bytes 294920 | tf_op jit(solution)/shard_map/ppermute | solution.py:16
  160.0 90.0 %all-gather.14.cloned.1.call-start = ((), (), s32[]{:S(2)}) async-start(), calls=%async_computation.3 | async-start | bytes 1671168 | tf_op jit(solution)/shard_map/all_gather | solution.py:90
  160.8 6.3 %collective-permute-start.2 = (bf16[384,128]{0,1:T(8,128)(2,1)S(1)}, bf16[384,128]{0,1:T(8,128)(2,1)S(1)}, u32[]{:S(2)}, u32[]{:S(2)}) collective-permute-start(bf16[384,128]{0,1:T(8,128)(2,1)S(1)} %copy-done.34), channel_id=1, source_target_pairs={{16,0},{32,16},{48,32},{64,48},{80,64},{96,80},{112,96},{17,1},{33... | collective-permute-start | bytes 294920 | tf_op jit(solution)/shard_map/ppermute | solution.py:16
  162.1 5.8 %collective-permute-start.4 = (bf16[24,128,2]{1,0,2:T(8,128)(2,1)S(1)}, bf16[24,128,2]{1,0,2:T(8,128)(2,1)S(1)}, u32[]{:S(2)}, u32[]{:S(2)}) collective-permute-start(bf16[24,128,2]{1,0,2:T(8,128)(2,1)S(1)} %get-tuple-element.30), channel_id=1, source_target_pairs={{0,1},{1,2},{2,3},{3,4},{4,5},{5,6},{6,7},{7,8},{8,9},{9,10},{10,1... | collective-permute-start | bytes 36872 | tf_op jit(solution)/shard_map/ppermute | solution.py:24
  165.2 5.0 %collective-permute-start.5 = (bf16[24,128,2]{1,0,2:T(8,128)(2,1)S(1)}, bf16[24,128,2]{1,0,2:T(8,128)(2,1)S(1)}, u32[]{:S(2)}, u32[]{:S(2)}) collective-permute-start(bf16[24,128,2]{1,0,2:T(8,128)(2,1)S(1)} %get-tuple-element.31), channel_id=1, source_target_pairs={{1,0},{2,1},{3,2},{4,3},{5,4},{6,5},{7,6},{8,7},{9,8},{10,9},{11,1... | collective-permute-start | bytes 36872 | tf_op jit(solution)/shard_map/ppermute | solution.py:27
  167.8 132.1 %all-gather.16.cloned.1.call-start = ((), (), s32[]{:S(2)}) async-start(), calls=%async_computation.4 | async-start | bytes 1671168 | tf_op jit(solution)/shard_map/all_gather | solution.py:89
  207.8 34.1 %collective-permute-start.3 = (bf16[384,128]{0,1:T(8,128)(2,1)S(1)}, bf16[384,128]{0,1:T(8,128)(2,1)}, u32[]{:S(2)}, u32[]{:S(2)}) collective-permute-start(bf16[384,128]{0,1:T(8,128)(2,1)S(1)} %fusion.161), channel_id=1, source_target_pairs={{0,16},{16,32},{32,48},{48,64},{64,80},{80,96},{96,112},{1,17},{17... | collective-permute-start | bytes 294920 | tf_op jit(solution)/shard_map/ppermute | solution.py:16
  255.8 90.3 %all-gather.18.cloned.1.call-start = ((), (), s32[]{:S(2)}) async-start(), calls=%async_computation.5 | async-start | bytes 1671168 | tf_op jit(solution)/shard_map/all_gather | solution.py:90
  255.9 6.4 %collective-permute-start.6 = (bf16[384,128]{0,1:T(8,128)(2,1)}, bf16[384,128]{0,1:T(8,128)(2,1)}, u32[]{:S(2)}, u32[]{:S(2)}) collective-permute-start(bf16[384,128]{0,1:T(8,128)(2,1)} %pad_maximum_fusion.8), channel_id=1, source_target_pairs={{16,0},{32,16},{48,32},{64,48},{80,64},{96,80},{112,96},{17,1},{33... | collective-permute-start | bytes 294920 | tf_op jit(solution)/shard_map/ppermute | solution.py:16
  262.3 133.7 %all-gather.20.cloned.1.call-start = ((), (), s32[]{:S(2)}) async-start(), calls=%async_computation.6 | async-start | bytes 1671168 | tf_op jit(solution)/shard_map/all_gather | solution.py:89
  264.1 4.8 %collective-permute-start.8 = (bf16[24,128,2]{1,0,2:T(8,128)(2,1)S(1)}, bf16[24,128,2]{1,0,2:T(8,128)(2,1)S(1)}, u32[]{:S(2)}, u32[]{:S(2)}) collective-permute-start(bf16[24,128,2]{1,0,2:T(8,128)(2,1)S(1)} %get-tuple-element.28), channel_id=1, source_target_pairs={{0,1},{1,2},{2,3},{3,4},{4,5},{5,6},{6,7},{7,8},{8,9},{9,10},{10,1... | collective-permute-start | bytes 36872 | tf_op jit(solution)/shard_map/ppermute | solution.py:24
  266.9 5.0 %collective-permute-start.9 = (bf16[24,128,2]{1,0,2:T(8,128)(2,1)S(1)}, bf16[24,128,2]{1,0,2:T(8,128)(2,1)S(1)}, u32[]{:S(2)}, u32[]{:S(2)}) collective-permute-start(bf16[24,128,2]{1,0,2:T(8,128)(2,1)S(1)} %get-tuple-element.29), channel_id=1, source_target_pairs={{1,0},{2,1},{3,2},{4,3},{5,4},{6,5},{7,6},{8,7},{9,8},{10,9},{11,1... | collective-permute-start | bytes 36872 | tf_op jit(solution)/shard_map/ppermute | solution.py:27
  304.5 41.6 %collective-permute-start.7 = (bf16[384,128]{0,1:T(8,128)(2,1)}, bf16[384,128]{0,1:T(8,128)(2,1)}, u32[]{:S(2)}, u32[]{:S(2)}) collective-permute-start(bf16[384,128]{0,1:T(8,128)(2,1)} %fusion.160), channel_id=1, source_target_pairs={{0,16},{16,32},{32,48},{48,64},{64,80},{80,96},{96,112},{1,17},{17... | collective-permute-start | bytes 294920 | tf_op jit(solution)/shard_map/ppermute | solution.py:16
  351.9 90.3 %all-gather.22.cloned.1.call-start = ((), (), s32[]{:S(2)}) async-start(), calls=%async_computation.7 | async-start | bytes 1671168 | tf_op jit(solution)/shard_map/all_gather | solution.py:90
  353.8 4.3 collective-permute-start.12
  355.7 5.0 %collective-permute-start.13 = (bf16[24,128,2]{1,0,2:T(8,128)(2,1)S(1)}, bf16[24,128,2]{1,0,2:T(8,128)(2,1)S(1)}, u32[]{:S(2)}, u32[]{:S(2)}) collective-permute-start(bf16[24,128,2]{1,0,2:T(8,128)(2,1)S(1)} %get-tuple-element.27), channel_id=1, source_target_pairs={{1,0},{2,1},{3,2},{4,3},{5,4},{6,5},{7,6},{8,7},{9,8},{10,9},{11,1... | collective-permute-start | bytes 36872 | tf_op jit(solution)/shard_map/ppermute | solution.py:27
  367.5 6.5 %collective-permute-start.10 = (bf16[384,128]{0,1:T(8,128)(2,1)S(1)}, bf16[384,128]{0,1:T(8,128)(2,1)S(1)}, u32[]{:S(2)}, u32[]{:S(2)}) collective-permute-start(bf16[384,128]{0,1:T(8,128)(2,1)S(1)} %copy-done.33), channel_id=1, source_target_pairs={{16,0},{32,16},{48,32},{64,48},{80,64},{96,80},{112,96},{17,1},{33... | collective-permute-start | bytes 294920 | tf_op jit(solution)/shard_map/ppermute | solution.py:16
  368.8 5.8 %collective-permute-start.14 = (bf16[24,128,2]{1,0,2:T(8,128)(2,1)S(1)}, bf16[24,128,2]{1,0,2:T(8,128)(2,1)S(1)}, u32[]{:S(2)}, u32[]{:S(2)}) collective-permute-start(bf16[24,128,2]{1,0,2:T(8,128)(2,1)S(1)} %get-tuple-element.24), channel_id=1, source_target_pairs={{0,1},{1,2},{2,3},{3,4},{4,5},{5,6},{6,7},{7,8},{8,9},{9,10},{10,1... | collective-permute-start | bytes 36872 | tf_op jit(solution)/shard_map/ppermute | solution.py:24
  370.8 5.0 %collective-permute-start.15 = (bf16[24,128,2]{1,0,2:T(8,128)(2,1)S(1)}, bf16[24,128,2]{1,0,2:T(8,128)(2,1)S(1)}, u32[]{:S(2)}, u32[]{:S(2)}) collective-permute-start(bf16[24,128,2]{1,0,2:T(8,128)(2,1)S(1)} %get-tuple-element.25), channel_id=1, source_target_pairs={{1,0},{2,1},{3,2},{4,3},{5,4},{6,5},{7,6},{8,7},{9,8},{10,9},{11,1... | collective-permute-start | bytes 36872 | tf_op jit(solution)/shard_map/ppermute | solution.py:27
  400.6 37.8 %collective-permute-start.11 = (bf16[384,128]{0,1:T(8,128)(2,1)}, bf16[384,128]{0,1:T(8,128)(2,1)}, u32[]{:S(2)}, u32[]{:S(2)}) collective-permute-start(bf16[384,128]{0,1:T(8,128)(2,1)} %fusion.159), channel_id=1, source_target_pairs={{0,16},{16,32},{32,48},{48,64},{64,80},{80,96},{96,112},{1,17},{17... | collective-permute-start | bytes 294920 | tf_op jit(solution)/shard_map/ppermute | solution.py:16
  403.6 24.9 %copy-start.18 = (bf16[24,128,128]{1,0,2:T(8,128)(2,1)S(1)}, bf16[24,128,128]{1,0,2:T(8,128)(2,1)}, u32[]{:S(2)}) copy-start(bf16[24,128,128]{1,0,2:T(8,128)(2,1)} %copy-done.17) | copy-start | bytes 2359300
  405.3 23.2 %copy-start.1 = (f32[24,128,132]{1,0,2:T(8,128)S(1)}, f32[24,128,132]{1,0,2:T(8,128)}, u32[]{:S(2)}) copy-start(f32[24,128,132]{1,0,2:T(8,128)} %copy-done) | copy-start | bytes 4866052
  405.3 23.2 %slice-start.2 = ((f32[24,128,132]{1,0,2:T(8,128)}), f32[24,128,130]{1,0,2:T(8,128)S(1)}, s32[]{:S(2)}) async-start(f32[24,128,132]{1,0,2:T(8,128)} %copy-done), calls=%async_computation.11 | async-start | bytes 3194880 | tf_op jit(solution)/shard_map/slice | solution.py:106
  (40 other events, 197.3 us)
Sparse Core Ops, SparseCore 0:
  11.1 89.5 all-gather.23
  103.1 51.1 all-gather.9
  160.1 43.6 all-gather.11
  206.0 43.9 all-gather.13
  256.0 43.9 all-gather.15
  302.0 44.0 all-gather.17
  352.1 43.9 all-gather.19
  398.3 43.9 all-gather.21
where the time goes:
time: 456 us; the launch traced here: 454 us
  waiting for transfers between devices  178 us (39%)
  blocking collectives  96.3 us (21%)
  matrix products  62.3 us (14%)
  starting transfers between devices  45.7 us (10%)
  other arithmetic  29.9 us (7%)
  local copies, waits for them, and re-layouts  26.8 us (6%)
  between operations  15 us (3%)
    all_gather x4, blocking collectives, from_root(): lax.all_gather(x, axis)  96.3 us
    all_gather x4, waiting for transfers between devices, per_device(): own_piece = lax.all_gather(rounded, 'row', axis=0, tiled=True)  78 us
    ppermute x8, waiting for transfers between devices, shifted(): return lax.ppermute(x, axis, pairs)  67.2 us
    all_gather x4, waiting for transfers between devices, per_device(): upper_piece = lax.all_gather(from_above, 'row', axis=0, tiled=True)  24 us
    unnamed x97, local copies, waits for them, and re-layouts  19.7 us
    ppermute x8, starting transfers between devices, shifted(): return lax.ppermute(x, axis, pairs)  17.6 us
    dot_general x4, matrix products, per_device(): jnp.dot(dipole_rows, upper_piece, preferred_element_type=jnp.float32)  17.4 us
    dot_general x4, matrix products, per_device(): lax.dot_general(dipole_cols, own_piece, (((0,), (0,)), ((), ())), preferr...  17.2 us
  transfers between devices with their start and end apart: 25, of which 14 were waited for; matrix products, arithmetic and copies ran while one was open for 19% of the time, Pallas kernels for 0%

commit v1 on v0

--- a/solution.py
+++ b/solution.py
@@ -86,8 +86,13 @@
     for order in range(1, TERMS + 1):
         rounded = inner_vec.astype(jnp.bfloat16)
         from_above = shifted(rounded, "sym", -1)
-        own_piece = lax.all_gather(rounded, "row", axis=0, tiled=True)
-        upper_piece = lax.all_gather(from_above, "row", axis=0, tiled=True)
+        own_piece, upper_piece = jnp.split(
+            lax.all_gather(
+                jnp.concatenate([rounded, from_above], axis=1), "row", axis=0, tiled=True
+            ),
+            [rounded.shape[1]],
+            axis=1,
+        )
         hamiltonian_part = jnp.dot(hamiltonian_rows, own_piece, preferred_element_type=jnp.float32)
         upper_part = jnp.dot(dipole_rows, upper_piece, preferred_element_type=jnp.float32)
         weighted = channel_hot[None, :, :] * ghost_rows[:, :, None]

time: 456 us -> 472 us (1.035)
  waiting for transfers between devices: 178 us -> 211 us
  matrix products: 62.3 us -> 53.5 us
  blocking collectives: 96.3 us -> 91.3 us
    all_to_all x1, waiting for transfers between devices: 0.01 us -> 65.7 us  [per_device(): lax.all_to_all(dipole_rows, 'row', split_axis=1, concat_axis=0, tiled=True)]
    ppermute x8, waiting for transfers between devices: 67.2 us -> 21.5 us  [shifted(): return lax.ppermute(x, axis, pairs)]
    all_gather x8 -> x4, waiting for transfers between devices: 102 us -> 112 us  [per_device(): lax.all_gather(jnp.concatenate([rounded, from_above], axis=1), 'row', axi...]
    dot_general x4, matrix products: 15 us -> 8.47 us  [per_device(): jnp.dot(hamiltonian_rows, own_piece, preferred_element_type=jnp.float32)]
    all_gather x4, blocking collectives: 96.3 us -> 91.3 us  [from_root(): lax.all_gather(x, axis)]
    unnamed x97 -> x99, local copies, waits for them, and re-layouts: 19.7 us -> 19.8 us
  transfers between devices with their start and end apart: 25 -> 21, of which waited for: 14 -> 14; matrix products, arithmetic and copies ran while one was open for 19% -> 11% of each run, Pallas kernels for 0% -> 0%
where the time goes in v1:
time: 472 us; the launch traced here: 470 us
  waiting for transfers between devices  211 us (45%)
  blocking collectives  91.3 us (19%)
  matrix products  53.5 us (11%)
  starting transfers between devices  43.4 us (9%)
  other arithmetic  29.8 us (6%)
  local copies, waits for them, and re-layouts  26.8 us (6%)
  between operations  14.8 us (3%)
    all_gather x4, waiting for transfers between devices, per_device(): lax.all_gather(jnp.concatenate([rounded, from_above], axis=1), 'row', axi...  112 us
    all_gather x4, blocking collectives, from_root(): lax.all_gather(x, axis)  91.3 us
    all_to_all x1, waiting for transfers between devices, per_device(): lax.all_to_all(dipole_rows, 'row', split_axis=1, concat_axis=0, tiled=True)  65.7 us
    ppermute x8, waiting for transfers between devices, shifted(): return lax.ppermute(x, axis, pairs)  21.5 us
    unnamed x99, local copies, waits for them, and re-layouts  19.8 us
    dot_general x4, matrix products, per_device(): lax.dot_general(dipole_cols, own_piece, (((0,), (0,)), ((), ())), preferr...  16.4 us
    dot_general x4, matrix products, per_device(): jnp.dot(dipole_rows, upper_piece, preferred_element_type=jnp.float32)  15.4 us
    ppermute x8, starting transfers between devices, shifted(): return lax.ppermute(x, axis, pairs)  14.1 us
  transfers between devices with their start and end apart: 21, of which 14 were waited for; matrix products, arithmetic and copies ran while one was open for 11% of the time, Pallas kernels for 0%

profile of v1, /device:TPU:1, one launch (start us, length us, event | category | flops | bytes accessed | tf_op | source)
XLA Modules:
  0.0 470.3 jit_solution(11498990812096394608)
XLA Ops:
  9.5 4.6 collective-permute-done
  14.8 6.6 %copy.38 = bf16[1,384,6144]{1,2,0:T(8,128)(2,1)} copy(bf16[1,384,6144]{2,1,0:T(8,128)(2,1)} %param.13) | data formatting | bytes 9437184 | tf_op args[3]
  21.5 10.0 %all-to-all-start = ((bf16[384,16,384]{0,2,1:T(8,128)(2,1)}), bf16[384,16,384]{0,2,1:T(8,128)(2,1)}, u32[]{:S(2)}, u32[]{:S(2)}) async-start(bf16[384,16,384]{0,2,1:T(8,128)(2,1)} %bitcast.248), calls=%async_computation | async-start | bytes 9437184 | tf_op jit(solution)/shard_map/all_to_all | solution.py:81
  33.8 65.7 %all-to-all-done = bf16[384,16,384]{0,2,1:T(8,128)(2,1)} async-done(((bf16[384,16,384]{0,2,1:T(8,128)(2,1)}), bf16[384,16,384]{0,2,1:T(8,128)(2,1)}, u32[]{:S(2)}, u32[]{:S(2)}) %all-to-all-start) | async-done | bytes 4718624 | tf_op jit(solution)/shard_map/all_to_all | solution.py:81
  99.5 6.6 %copy.39 = bf16[16,384,384]{2,1,0:T(8,128)(2,1)} copy(bf16[16,384,384]{1,2,0:T(8,128)(2,1)} %bitcast.7) | data formatting | bytes 9437184 | tf_op jit(solution)/shard_map/all_to_all | solution.py:81
  106.1 7.8 %all-gather.5.cloned.1.call-done = bf16[6144,256]{1,0:T(8,128)(2,1)} async-done(((bf16[384,256]{1,0:T(8,128)(2,1)}), bf16[6144,256]{1,0:T(8,128)(2,1)}) %all-gather.5.cloned.1.call-update) | async-done | bytes 3145744 | tf_op jit(solution)/shard_map/all_gather | solution.py:90
  116.3 24.6 %all_gather.29 = f32[16,24,128]{2,1,0:T(8,128)S(1)} all-gather(f32[1,24,128]{2,1,0:T(8,128)S(1)} %get-tuple-element.56), channel_id=1, replica_groups=mesh['sym'=8,'row'=16] {'row'}, dimensions={0}, use_global_device_ids=true | all-gather | bytes 208896 | tf_op jit(solution)/shard_map/all_gather | solution.py:33
  140.9 4.0 fusion.253
  148.5 3.9 fusion.216
  155.9 5.2 %collective-permute-done.2 = bf16[384,128]{0,1:T(8,128)(2,1)S(1)} collective-permute-done((bf16[384,128]{0,1:T(8,128)(2,1)S(1)}, bf16[384,128]{0,1:T(8,128)(2,1)S(1)}, u32[]{:S(2)}, u32[]{:S(2)}) %collective-permute-start.2) | collective-permute-done | bytes 98336 | tf_op jit(solution)/shard_map/ppermute | solution.py:16
  173.7 42.9 %all-gather.7.cloned.1.call-done = bf16[6144,256]{0,1:T(8,128)(2,1)} async-done(((bf16[384,256]{0,1:T(8,128)(2,1)}), bf16[6144,256]{0,1:T(8,128)(2,1)}) %all-gather.7.cloned.1.call-update) | async-done | bytes 3145744 | tf_op jit(solution)/shard_map/all_gather | solution.py:90
  216.5 3.9 fusion.256
  222.9 3.3 fusion.20
  226.2 22.4 %all_gather.31 = f32[16,24,128]{2,1,0:T(8,128)S(1)} all-gather(f32[1,24,128]{2,1,0:T(8,128)S(1)} %get-tuple-element.53), channel_id=1, replica_groups=mesh['sym'=8,'row'=16] {'row'}, dimensions={0}, use_global_device_ids=true | all-gather | bytes 208896 | tf_op jit(solution)/shard_map/all_gather | solution.py:33
  248.9 3.8 fusion.206
  256.3 4.8 %collective-permute-done.6 = bf16[384,128]{0,1:T(8,128)(2,1)S(1)} collective-permute-done((bf16[384,128]{0,1:T(8,128)(2,1)S(1)}, bf16[384,128]{0,1:T(8,128)(2,1)S(1)}, u32[]{:S(2)}, u32[]{:S(2)}) %collective-permute-start.6) | collective-permute-done | bytes 98336 | tf_op jit(solution)/shard_map/ppermute | solution.py:16
  263.7 2.9 collective-permute-start.8
  268.6 3.1 collective-permute-done.9
  277.3 36.8 %all-gather.9.cloned.1.call-done = bf16[6144,256]{0,1:T(8,128)(2,1)} async-done(((bf16[384,256]{0,1:T(8,128)(2,1)}), bf16[6144,256]{0,1:T(8,128)(2,1)}) %all-gather.9.cloned.1.call-update) | async-done | bytes 3145744 | tf_op jit(solution)/shard_map/all_gather | solution.py:90
  314.1 3.9 fusion.259
  320.4 3.3 fusion.18
  323.8 22.2 %all_gather.33 = f32[16,24,128]{2,1,0:T(8,128)S(1)} all-gather(f32[1,24,128]{2,1,0:T(8,128)S(1)} %get-tuple-element.50), channel_id=1, replica_groups=mesh['sym'=8,'row'=16] {'row'}, dimensions={0}, use_global_device_ids=true | all-gather | bytes 208896 | tf_op jit(solution)/shard_map/all_gather | solution.py:33
  346.3 3.8 fusion.196
  353.7 4.8 %collective-permute-done.10 = bf16[384,128]{0,1:T(8,128)(2,1)S(1)} collective-permute-done((bf16[384,128]{0,1:T(8,128)(2,1)S(1)}, bf16[384,128]{0,1:T(8,128)(2,1)S(1)}, u32[]{:S(2)}, u32[]{:S(2)}) %collective-permute-start.10) | collective-permute-done | bytes 98336 | tf_op jit(solution)/shard_map/ppermute | solution.py:16
  361.0 2.9 collective-permute-start.12
  386.5 24.9 %all-gather.11.cloned.1.call-done = bf16[6144,256]{0,1:T(8,128)(2,1)} async-done(((bf16[384,256]{0,1:T(8,128)(2,1)}), bf16[6144,256]{0,1:T(8,128)(2,1)}) %all-gather.11.cloned.1.call-update) | async-done | bytes 3145744 | tf_op jit(solution)/shard_map/all_gather | solution.py:90
  411.4 4.6 fusion.262
  416.0 3.0 collective-permute-start.11
  420.7 22.2 %all_gather.35 = f32[16,24,128]{2,1,0:T(8,128)S(1)} all-gather(f32[1,24,128]{2,1,0:T(8,128)S(1)} %get-tuple-element.47), channel_id=1, replica_groups=mesh['sym'=8,'row'=16] {'row'}, dimensions={0}, use_global_device_ids=true | all-gather | bytes 208896 | tf_op jit(solution)/shard_map/all_gather | solution.py:33
  451.7 3.2 copy.47
  454.9 3.9 fusion.186
  458.9 3.9 fusion.236
  (196 shorter events, 86.1 us)
Async XLA Ops:
  7.2 106.7 %all-gather.5.cloned.1.call-start = ((), (), s32[]{:S(2)}) async-start(), calls=%async_computation.1 | async-start | bytes 3342336 | tf_op jit(solution)/shard_map/all_gather | solution.py:90
  8.2 5.9 %collective-permute-start = (bf16[384,128]{1,0:T(8,128)(2,1)S(1)}, bf16[384,128]{1,0:T(8,128)(2,1)S(1)}, u32[]{:S(2)}, u32[]{:S(2)}) collective-permute-start(bf16[384,128]{1,0:T(8,128)(2,1)S(1)} %convert_bitcast_fusion), channel_id=1, source_target_pairs={{16,0},{32,16},{48,32},{64,48},{80,64},{96,80},{112,96},{17,1},{33... | collective-permute-start | bytes 294920 | tf_op jit(solution)/shard_map/ppermute | solution.py:16
  21.5 78.0 %all-to-all-start = ((bf16[384,16,384]{0,2,1:T(8,128)(2,1)}), bf16[384,16,384]{0,2,1:T(8,128)(2,1)}, u32[]{:S(2)}, u32[]{:S(2)}) async-start(bf16[384,16,384]{0,2,1:T(8,128)(2,1)} %bitcast.248), calls=%async_computation | async-start | bytes 9437184 | tf_op jit(solution)/shard_map/all_to_all | solution.py:81
  31.4 185.1 %all-gather.7.cloned.1.call-start = ((), (), s32[]{:S(2)}) async-start(), calls=%async_computation.2 | async-start | bytes 3342336 | tf_op jit(solution)/shard_map/all_gather | solution.py:90
  33.8 80.1 %copy-start.10 = (f32[6144,24]{0,1:T(8,128)}, f32[6144,24]{0,1:T(8,128)S(1)}, u32[]{:S(2)}) copy-start(f32[6144,24]{0,1:T(8,128)S(1)} %get-tuple-element.58) | copy-start | bytes 1769476
  33.8 312.2 %copy-start.37 = (pred[6144,24]{0,1:T(8,128)(4,1)}, pred[6144,24]{0,1:T(8,128)(4,1)S(1)}, u32[]{:S(2)}) copy-start(pred[6144,24]{0,1:T(8,128)(4,1)S(1)} %get-tuple-element.57) | copy-start | bytes 442372
  113.9 38.5 %slice-start = ((s8[4718592]{0:T(1024)(128)(4,1)}), s8[4194304]{0:T(1024)(128)(4,1)S(1)}, s32[]{:S(2)}) async-start(s8[4718592]{0:T(1024)(128)(4,1)} %bitcast.241), calls=%async_computation.5 | async-start | bytes 8388608
  144.9 3.6 collective-permute-start.1
  154.6 6.5 %collective-permute-start.2 = (bf16[384,128]{0,1:T(8,128)(2,1)S(1)}, bf16[384,128]{0,1:T(8,128)(2,1)S(1)}, u32[]{:S(2)}, u32[]{:S(2)}) collective-permute-start(bf16[384,128]{0,1:T(8,128)(2,1)S(1)} %pad_maximum_fusion.11), channel_id=1, source_target_pairs={{16,0},{32,16},{48,32},{64,48},{80,64},{96,80},{112,96},{17,1},{33... | collective-permute-start | bytes 294920 | tf_op jit(solution)/shard_map/ppermute | solution.py:16
  161.8 152.2 %all-gather.9.cloned.1.call-start = ((), (), s32[]{:S(2)}) async-start(), calls=%async_computation.3 | async-start | bytes 3342336 | tf_op jit(solution)/shard_map/all_gather | solution.py:90
  162.0 5.2 %collective-permute-start.4 = (bf16[24,128,2]{1,0,2:T(8,128)(2,1)S(1)}, bf16[24,128,2]{1,0,2:T(8,128)(2,1)S(1)}, u32[]{:S(2)}, u32[]{:S(2)}) collective-permute-start(bf16[24,128,2]{1,0,2:T(8,128)(2,1)S(1)} %get-tuple-element.30), channel_id=1, source_target_pairs={{0,1},{1,2},{2,3},{3,4},{4,5},{5,6},{6,7},{7,8},{8,9},{9,10},{10,1... | collective-permute-start | bytes 36872 | tf_op jit(solution)/shard_map/ppermute | solution.py:24
  164.4 5.0 %collective-permute-start.5 = (bf16[24,128,2]{1,0,2:T(8,128)(2,1)S(1)}, bf16[24,128,2]{1,0,2:T(8,128)(2,1)S(1)}, u32[]{:S(2)}, u32[]{:S(2)}) collective-permute-start(bf16[24,128,2]{1,0,2:T(8,128)(2,1)S(1)} %get-tuple-element.31), channel_id=1, source_target_pairs={{1,0},{2,1},{3,2},{4,3},{5,4},{6,5},{7,6},{8,7},{9,8},{10,9},{11,1... | collective-permute-start | bytes 36872 | tf_op jit(solution)/shard_map/ppermute | solution.py:27
  216.5 36.2 %slice-start.2 = ((s8[4718592]{0:T(1024)(128)(4,1)}), s8[4194304]{0:T(1024)(128)(4,1)S(1)}, s32[]{:S(2)}) async-start(s8[4718592]{0:T(1024)(128)(4,1)} %bitcast.243), calls=%async_computation.7 | async-start | bytes 8388608
  220.5 28.4 %collective-permute-start.3 = (bf16[384,128]{0,1:T(8,128)(2,1)S(1)}, bf16[384,128]{0,1:T(8,128)(2,1)S(1)}, u32[]{:S(2)}, u32[]{:S(2)}) collective-permute-start(bf16[384,128]{0,1:T(8,128)(2,1)S(1)} %fusion.256), channel_id=1, source_target_pairs={{0,16},{16,32},{32,48},{48,64},{64,80},{80,96},{96,112},{1,17},{17... | collective-permute-start | bytes 294920 | tf_op jit(solution)/shard_map/ppermute | solution.py:16
  222.9 26.1 %copy-start.17 = (bf16[6144,256]{0,1:T(8,128)(2,1)S(1)}, bf16[6144,256]{0,1:T(8,128)(2,1)}, u32[]{:S(2)}) copy-start(bf16[6144,256]{0,1:T(8,128)(2,1)} %all-gather.7.cloned.1.call-done) | copy-start | bytes 9437188
  226.1 26.6 %slice-start.3 = ((s8[4718592]{0:T(1024)(128)(4,1)}), s8[524288]{0:T(1024)(128)(4,1)S(1)}, s32[]{:S(2)}) async-start(s8[4718592]{0:T(1024)(128)(4,1)} %bitcast.243), calls=%async_computation.8 | async-start | bytes 1048576
  255.0 6.1 %collective-permute-start.6 = (bf16[384,128]{0,1:T(8,128)(2,1)S(1)}, bf16[384,128]{0,1:T(8,128)(2,1)S(1)}, u32[]{:S(2)}, u32[]{:S(2)}) collective-permute-start(bf16[384,128]{0,1:T(8,128)(2,1)S(1)} %pad_maximum_fusion.12), channel_id=1, source_target_pairs={{16,0},{32,16},{48,32},{64,48},{80,64},{96,80},{112,96},{17,1},{33... | collective-permute-start | bytes 294920 | tf_op jit(solution)/shard_map/ppermute | solution.py:16
  261.9 149.5 %all-gather.11.cloned.1.call-start = ((), (), s32[]{:S(2)}) async-start(), calls=%async_computation.4 | async-start | bytes 3342336 | tf_op jit(solution)/shard_map/all_gather | solution.py:90
  263.7 4.8 %collective-permute-start.8 = (bf16[24,128,2]{1,0,2:T(8,128)(2,1)S(1)}, bf16[24,128,2]{1,0,2:T(8,128)(2,1)S(1)}, u32[]{:S(2)}, u32[]{:S(2)}) collective-permute-start(bf16[24,128,2]{1,0,2:T(8,128)(2,1)S(1)} %get-tuple-element.28), channel_id=1, source_target_pairs={{0,1},{1,2},{2,3},{3,4},{4,5},{5,6},{6,7},{7,8},{8,9},{9,10},{10,1... | collective-permute-start | bytes 36872 | tf_op jit(solution)/shard_map/ppermute | solution.py:24
  266.6 5.0 %collective-permute-start.9 = (bf16[24,128,2]{1,0,2:T(8,128)(2,1)S(1)}, bf16[24,128,2]{1,0,2:T(8,128)(2,1)S(1)}, u32[]{:S(2)}, u32[]{:S(2)}) collective-permute-start(bf16[24,128,2]{1,0,2:T(8,128)(2,1)S(1)} %get-tuple-element.29), channel_id=1, source_target_pairs={{1,0},{2,1},{3,2},{4,3},{5,4},{6,5},{7,6},{8,7},{9,8},{10,9},{11,1... | collective-permute-start | bytes 36872 | tf_op jit(solution)/shard_map/ppermute | solution.py:27
  314.1 36.1 %slice-start.4 = ((s8[4718592]{0:T(1024)(128)(4,1)}), s8[4194304]{0:T(1024)(128)(4,1)S(1)}, s32[]{:S(2)}) async-start(s8[4718592]{0:T(1024)(128)(4,1)} %bitcast.245), calls=%async_computation.9 | async-start | bytes 8388608
  318.0 28.2 %collective-permute-start.7 = (bf16[384,128]{0,1:T(8,128)(2,1)S(1)}, bf16[384,128]{0,1:T(8,128)(2,1)S(1)}, u32[]{:S(2)}, u32[]{:S(2)}) collective-permute-start(bf16[384,128]{0,1:T(8,128)(2,1)S(1)} %fusion.259), channel_id=1, source_target_pairs={{0,16},{16,32},{32,48},{48,64},{64,80},{80,96},{96,112},{1,17},{17... | collective-permute-start | bytes 294920 | tf_op jit(solution)/shard_map/ppermute | solution.py:16
  320.4 25.9 %copy-start.18 = (bf16[6144,256]{0,1:T(8,128)(2,1)S(1)}, bf16[6144,256]{0,1:T(8,128)(2,1)}, u32[]{:S(2)}) copy-start(bf16[6144,256]{0,1:T(8,128)(2,1)} %all-gather.9.cloned.1.call-done) | copy-start | bytes 9437188
  323.7 26.5 %slice-start.5 = ((s8[4718592]{0:T(1024)(128)(4,1)}), s8[524288]{0:T(1024)(128)(4,1)S(1)}, s32[]{:S(2)}) async-start(s8[4718592]{0:T(1024)(128)(4,1)} %bitcast.245), calls=%async_computation.10 | async-start | bytes 1048576
  352.4 6.1 %collective-permute-start.10 = (bf16[384,128]{0,1:T(8,128)(2,1)S(1)}, bf16[384,128]{0,1:T(8,128)(2,1)S(1)}, u32[]{:S(2)}, u32[]{:S(2)}) collective-permute-start(bf16[384,128]{0,1:T(8,128)(2,1)S(1)} %pad_maximum_fusion.13), channel_id=1, source_target_pairs={{16,0},{32,16},{48,32},{64,48},{80,64},{96,80},{112,96},{17,1},{33... | collective-permute-start | bytes 294920 | tf_op jit(solution)/shard_map/ppermute | solution.py:16
  361.0 5.1 %collective-permute-start.12 = (bf16[24,128,2]{1,0,2:T(8,128)(2,1)S(1)}, bf16[24,128,2]{1,0,2:T(8,128)(2,1)S(1)}, u32[]{:S(2)}, u32[]{:S(2)}) collective-permute-start(bf16[24,128,2]{1,0,2:T(8,128)(2,1)S(1)} %get-tuple-element.26), channel_id=1, source_target_pairs={{0,1},{1,2},{2,3},{3,4},{4,5},{5,6},{6,7},{7,8},{8,9},{9,10},{10,1... | collective-permute-start | bytes 36872 | tf_op jit(solution)/shard_map/ppermute | solution.py:24
  363.9 5.0 %collective-permute-start.13 = (bf16[24,128,2]{1,0,2:T(8,128)(2,1)S(1)}, bf16[24,128,2]{1,0,2:T(8,128)(2,1)S(1)}, u32[]{:S(2)}, u32[]{:S(2)}) collective-permute-start(bf16[24,128,2]{1,0,2:T(8,128)(2,1)S(1)} %get-tuple-element.27), channel_id=1, source_target_pairs={{1,0},{2,1},{3,2},{4,3},{5,4},{6,5},{7,6},{8,7},{9,8},{10,9},{11,1... | collective-permute-start | bytes 36872 | tf_op jit(solution)/shard_map/ppermute | solution.py:27
  376.7 4.5 collective-permute-start.14
  378.6 5.4 %collective-permute-start.15 = (bf16[24,128,2]{1,0,2:T(8,128)(2,1)S(1)}, bf16[24,128,2]{1,0,2:T(8,128)(2,1)S(1)}, u32[]{:S(2)}, u32[]{:S(2)}) collective-permute-start(bf16[24,128,2]{1,0,2:T(8,128)(2,1)S(1)} %get-tuple-element.25), channel_id=1, source_target_pairs={{1,0},{2,1},{3,2},{4,3},{5,4},{6,5},{7,6},{8,7},{9,8},{10,9},{11,1... | collective-permute-start | bytes 36872 | tf_op jit(solution)/shard_map/ppermute | solution.py:27
  416.0 38.9 %collective-permute-start.11 = (bf16[384,128]{0,1:T(8,128)(2,1)}, bf16[384,128]{0,1:T(8,128)(2,1)}, u32[]{:S(2)}, u32[]{:S(2)}) collective-permute-start(bf16[384,128]{0,1:T(8,128)(2,1)} %fusion.262), channel_id=1, source_target_pairs={{0,16},{16,32},{32,48},{48,64},{64,80},{80,96},{96,112},{1,17},{17... | collective-permute-start | bytes 294920 | tf_op jit(solution)/shard_map/ppermute | solution.py:16
  418.9 24.0 %copy-start.20 = (bf16[24,128,128]{1,0,2:T(8,128)(2,1)S(1)}, bf16[24,128,128]{1,0,2:T(8,128)(2,1)}, u32[]{:S(2)}) copy-start(bf16[24,128,128]{1,0,2:T(8,128)(2,1)} %copy-done.19) | copy-start | bytes 2359300
  420.6 22.3 %copy-start.1 = (f32[24,128,132]{1,0,2:T(8,128)S(1)}, f32[24,128,132]{1,0,2:T(8,128)}, u32[]{:S(2)}) copy-start(f32[24,128,132]{1,0,2:T(8,128)} %copy-done) | copy-start | bytes 4866052
  (37 other events, 194.0 us)
Sparse Core Ops, SparseCore 0:
  14.9 98.8 all-gather.4
  162.0 54.5 all-gather.6
  262.0 51.9 all-gather.8
  359.4 51.9 all-gather.10
